TPU v7x, 32 devices: a whole 2x2x4 slice. The times are simulated.
32 devices in a mesh: dir: 8 (over z, y), near: 4 (over x, core).
Axes of the slice: x: 2, y: 2, z: 4, core: 2. Of those that a mesh axis runs over, the one named last changes fastest.
Arguments:
- currents: bfloat16 [1024, 128, 128], P(('dir', 'near')), may hold values from -6 to 6
- counts: int32 [32], replicated, may hold values from 0 to 4, as said below
- near_source: int32 [1024, 6], P(('dir', 'near')), may hold values from 0 to 1023, as said below
- near_blocks: bfloat16 [1024, 6, 128, 256], P(('dir', 'near')), may hold values from -0.15625 to 0.15625
- aggregate: bfloat16 [8, 1152, 256], replicated, may hold values from -0.125 to 0.125
- receive: bfloat16 [8, 128, 2304], replicated, may hold values from -0.125 to 0.125
- translations: bfloat16 [1, 1, 1152, 64, 128], P(None, None, ('dir', 'near')), may hold values from -0.5 to 0.5
- source_blocks: int32 [1, 1], replicated, may hold values from 0 to 0, as said below
Outputs:
- fields: bfloat16 [1024, 128, 128], P(('dir', 'near'))
Inputs may be any that keep to these rules, and one draw needn't show every extreme that they name: `counts`: devices 2 m and 2 m + 1 of dir and near together (neighbours along near) own exactly 4 parents between them; some device owns 4 and its neighbour none. `near_source`: every entry names a live leaf slot on the device of its row or on a device next to it along near with the same dir index. `source_blocks`: each row names 1 different blocks.
All inputs are finite; a program needn't handle non-finite values.
Results may differ from a plain program's by a relative error of at most 0.005.
Values may be sent and summed in bfloat16 or wider, within the bound.
A program may use at most 128 MiB of HBM per device.

v0:
```python
import functools

import jax
import jax.numpy as jnp
from jax import lax
from jax.experimental import pallas as pl
from jax.experimental.pallas import tpu as pltpu
from jax.sharding import PartitionSpec as P

MESH = pl.DeviceIdType.MESH
F32 = jnp.float32
BF16 = jnp.bfloat16


def turned(values):
    width = values.shape[-1]
    rolled = pltpu.roll(values, width // 2, values.ndim - 1)
    lane = lax.broadcasted_iota(jnp.int32, values.shape, values.ndim - 1)
    return jnp.where(lane < width // 2, -rolled, rolled)


def flipped(index, step, count):
    total = 0
    bit = 1
    while bit < count:
        total = total + bit * lax.rem(index // bit + step // bit, 2)
        bit *= 2
    return total


def kernel(
    dims,
    counts,
    near_source,
    source_blocks,
    currents,
    near_blocks,
    aggregate,
    receive,
    translations,
    out,
    own,
    borrowed,
    window,
    near_v,
    agg_v,
    rec_v,
    tra_v,
    stack,
    tile_rows,
    tile_pack,
    send1,
    recv1,
    gathered,
    incoming,
    send2,
    recv2,
    spread,
    joined,
    joined16,
    far_own,
    far_send,
    far_recv,
    near_acc,
    load_sem,
    pair_sem,
    halo_sem,
    a2a_sem,
    far_sem,
):
    dirs, nears, per, padded, slots, dirs_per_tile = dims
    devices = dirs * nears
    leaf_slots = own.shape[0]
    unknowns, channels = own.shape[1:]
    parent_slots = leaf_slots // 8
    half = parent_slots // 2
    near_per = near_v.shape[1]
    directions = agg_v.shape[1]
    dir_index = lax.axis_index("dir")
    near_index = lax.axis_index("near")
    me = dir_index * nears + near_index
    odd = lax.rem(near_index, 2)
    mate = near_index + 1 - 2 * odd
    half_leaves = half * 8

    load_own = pltpu.make_async_copy(currents, own, load_sem.at[0])
    load_agg = pltpu.make_async_copy(aggregate, agg_v, load_sem.at[1])
    load_mid = pltpu.make_async_copy(currents, window.at[pl.ds(leaf_slots, leaf_slots)], load_sem.at[2])
    load_tra = pltpu.make_async_copy(translations, tra_v, load_sem.at[3])
    load_rec = pltpu.make_async_copy(receive, rec_v, load_sem.at[4])
    load_near = pltpu.make_async_copy(near_blocks, near_v, load_sem.at[5])

    def start_pieces(source, target, sem, pieces):
        size = target.shape[0] // pieces
        for piece in range(pieces):
            cut = pl.ds(piece * size, size)
            pltpu.make_async_copy(source.at[cut], target.at[cut], sem).start()

    load_own.start()
    start_pieces(aggregate, agg_v, load_sem.at[1], 8)
    load_tra.start()
    load_mid.start()
    start_pieces(near_blocks, near_v, load_sem.at[5], 8)
    start_pieces(receive, rec_v, load_sem.at[4], 8)

    barrier = pltpu.get_barrier_semaphore()

    def greet(step, carry):
        other = flipped(me, devices - step, devices)
        pl.semaphore_signal(
            barrier, inc=1, device_id=(other // nears, lax.rem(other, nears)), device_id_type=MESH
        )
        return carry

    lax.fori_loop(1, devices, greet, 0, unroll=True)
    pl.semaphore_wait(barrier, devices - 1)

    to_mate = pltpu.make_async_remote_copy(
        src_ref=currents.at[pl.ds((1 - odd) * half_leaves, half_leaves)],
        dst_ref=borrowed,
        send_sem=pair_sem.at[0],
        recv_sem=pair_sem.at[1],
        device_id=(dir_index, mate),
        device_id_type=MESH,
    )
    to_mate.start()

    def halo(side, block):
        return pltpu.make_async_remote_copy(
            src_ref=currents,
            dst_ref=window.at[pl.ds(block * leaf_slots, leaf_slots)],
            send_sem=halo_sem.at[0, block // 2],
            recv_sem=halo_sem.at[1, block // 2],
            device_id=(dir_index, near_index + side),
            device_id_type=MESH,
        )

    @pl.when(near_index < nears - 1)
    def _():
        halo(1, 0).start()

    @pl.when(near_index > 0)
    def _():
        halo(-1, 2).start()

    own_count = counts[me]
    mate_count = counts[dir_index * nears + mate]
    even_count = jnp.where(odd == 0, own_count, mate_count)
    load_own.wait()
    to_mate.wait_recv()
    for w in range(half):
        is_own = jnp.where(odd == 0, w < own_count, half + w >= even_count)
        own_slot = jnp.clip(jnp.where(odd == 0, w, half + w - even_count), 0, parent_slots - 1)
        mate_slot = jnp.clip(jnp.where(odd == 0, w - own_count, w), 0, half - 1)
        for c in range(8):
            mine = own[own_slot * 8 + c].astype(F32)
            theirs = borrowed[mate_slot * 8 + c].astype(F32)
            stack[pl.ds(c * unknowns, unknowns), pl.ds(w * channels, channels)] = jnp.where(
                is_own, mine, theirs
            ).astype(BF16)
    load_agg.wait()

    def hop(buffer, target, other, phase):
        return pltpu.make_async_remote_copy(
            src_ref=buffer.at[other],
            dst_ref=target.at[me],
            send_sem=a2a_sem.at[phase, 0],
            recv_sem=a2a_sem.at[phase, 1],
            device_id=(other // nears, lax.rem(other, nears)),
            device_id_type=MESH,
        )

    def all_sent(buffer, phase, which):
        some = buffer.at[pl.ds(0, devices - 1)]
        pltpu.make_async_copy(some, some, a2a_sem.at[phase, which]).wait()

    message = send1.shape[1:]
    tile_devices = dirs_per_tile * nears
    tiles = devices // tile_devices
    rows = tile_devices * per
    block_rows = slots * padded

    def radiate(tile):
        start = pl.multiple_of(tile * rows, 16)
        parts = [agg_v[c, pl.ds(start, rows), :] for c in range(8)]
        real = jnp.concatenate([p[:, :unknowns] for p in parts], axis=1)
        imag = jnp.concatenate([p[:, unknowns:] for p in parts], axis=1)
        rhs = stack[...]
        real = jnp.dot(real, rhs, preferred_element_type=F32)
        imag = jnp.dot(imag, rhs, preferred_element_type=F32)
        for s in range(slots):
            lanes = slice(s * channels, (s + 1) * channels)
            tile_rows[s] = real[:, lanes] + turned(imag[:, lanes])
        for q in range(tile_devices):
            for s in range(slots):
                tile_pack[pl.ds(q * block_rows + s * padded, per), :] = tile_rows[
                    s, pl.ds(q * per, per), :
                ]
        for q in range(tile_devices):
            packed = tile_pack[pl.ds(q * block_rows, block_rows), :]
            send1[tile * tile_devices + q] = packed.reshape(message).astype(BF16)

    my_tile = me // tile_devices

    def radiate_and_send(step, carry):
        tile = flipped(my_tile, tiles - 1 - step, tiles)
        radiate(tile)
        for q in range(tile_devices):
            hop(send1, recv1, tile * tile_devices + q, 0).start()
        return carry

    lax.fori_loop(0, tiles - 1, radiate_and_send, 0)
    radiate(my_tile)
    for q in range(1, tile_devices):
        first = my_tile * tile_devices
        hop(send1, recv1, first + flipped(me - first, q, tile_devices), 0).start()
    recv1[me] = send1[me]

    all_sent(recv1, 0, 1)
    load_tra.wait()
    blocks, listed, _, block_size, doubled = tra_v.shape
    block_len = block_size * padded
    for b in range(blocks):
        per_block = devices // blocks
        got = recv1[pl.ds(b * per_block, per_block)].astype(F32)
        gathered[b] = got.reshape(block_len, channels)

    def translate(k, carry):
        for b in range(blocks):
            summed = None
            for l in range(listed):
                source = 0 if blocks == 1 else source_blocks[b, l]
                rows_k = gathered[source, pl.ds(k, block_size, stride=padded), :]
                both = jnp.concatenate([rows_k, turned(rows_k)], axis=0).astype(BF16)
                part = jnp.dot(tra_v[b, l, k], both, preferred_element_type=F32)
                summed = part if summed is None else summed + part
            incoming[b, pl.ds(k, block_size, stride=padded), :] = summed
        return carry

    lax.fori_loop(0, per, translate, 0, unroll=per % 4 == 0 and per or 1)
    for b in range(blocks):
        per_block = devices // blocks
        packed = incoming[b].reshape((per_block,) + message)
        send2[pl.ds(b * per_block, per_block)] = packed.astype(BF16)

    def send_back(step, carry):
        hop(send2, recv2, flipped(me, devices - 1 - step, devices), 1).start()
        return carry

    lax.fori_loop(0, devices - 1, send_back, 0, unroll=True)
    recv2[me] = send2[me]

    load_mid.wait()
    load_near.wait()

    @pl.when(near_index > 0)
    def _():
        halo(1, 0).wait_recv()

    @pl.when(near_index < nears - 1)
    def _():
        halo(-1, 2).wait_recv()

    base = (me - 1) * leaf_slots

    def nearby(i, carry):
        rows_at = [near_source[e, i] - base for e in range(near_per)]
        sources = [window[jnp.clip(r, 0, 3 * leaf_slots - 1)] for r in rows_at]
        parts = [near_v[i, e] for e in range(near_per)]
        real = jnp.concatenate([p[:, :unknowns] for p in parts], axis=1)
        imag = jnp.concatenate([p[:, unknowns:] for p in parts], axis=1)
        result = jnp.dot(
            jnp.concatenate([real, imag], axis=0),
            jnp.concatenate(sources, axis=0),
            preferred_element_type=F32,
        )
        near_acc[i] = result[:unknowns] + turned(result[unknowns:])
        return carry

    lax.fori_loop(0, leaf_slots, nearby, 0)

    all_sent(recv2, 1, 1)
    load_rec.wait()
    spread[...] = recv2[...].astype(F32).reshape(spread.shape)
    for d in range(devices):
        for s in range(slots):
            joined[pl.ds(d * per, per), pl.ds(s * channels, channels)] = spread[
                pl.ds(d * block_rows + s * padded, per), :
            ]
    joined16[...] = joined[...].astype(BF16)

    def far_copy(c):
        return pltpu.make_async_remote_copy(
            src_ref=far_send.at[c],
            dst_ref=far_recv.at[c],
            send_sem=far_sem.at[0, c],
            recv_sem=far_sem.at[1, c],
            device_id=(dir_index, mate),
            device_id_type=MESH,
        )

    def absorb(c, carry):
        fields = joined16[...]
        real = jnp.dot(rec_v[c, :, pl.ds(0, directions)], fields, preferred_element_type=F32)
        imag = jnp.dot(
            rec_v[c, :, pl.ds(directions, directions)], fields, preferred_element_type=F32
        )
        for s in range(slots):
            lanes = slice(s * channels, (s + 1) * channels)
            far = real[:, lanes] + turned(imag[:, lanes])
            far_own[c, s] = far
            far_send[c, s] = far.astype(BF16)
        far_copy(c).start()
        return carry

    lax.fori_loop(0, 8, absorb, 0)

    def finish(c, carry):
        far_copy(c).wait_recv()
        for s in range(parent_slots):
            place = jnp.where(odd == 0, s, even_count + s)
            mine_at = place - half * odd
            mine = (mine_at >= 0) & (mine_at < half)
            own_at = jnp.clip(mine_at, 0, half - 1)
            mate_at = jnp.clip(place - half * (1 - odd), 0, half - 1)
            theirs = far_recv[c, 0]
            for w in range(1, half):
                theirs = jnp.where(mate_at == w, far_recv[c, w], theirs)
            far = jnp.where(mine, far_own[c, own_at], theirs.astype(F32))
            total = far + near_acc[s * 8 + c]
            out[s * 8 + c] = jnp.where(s < own_count, total, 0.0).astype(BF16)
        return carry

    lax.fori_loop(0, 8, finish, 0)

    to_mate.wait_send()
    all_sent(send1, 0, 0)
    all_sent(send2, 1, 0)
    for c in range(8):
        far_copy(c).wait_send()

    @pl.when(near_index < nears - 1)
    def _():
        halo(1, 0).wait_send()

    @pl.when(near_index > 0)
    def _():
        halo(-1, 2).wait_send()


def body(
    currents, counts, near_source, near_blocks, aggregate, receive, translations, source_blocks
):
    dirs, nears = lax.axis_size("dir"), lax.axis_size("near")
    devices = dirs * nears
    leaf_slots, unknowns, channels = currents.shape
    parent_slots = leaf_slots // 8
    slots = parent_slots // 2
    blocks, listed, per, block_size, doubled = translations.shape
    directions = aggregate.shape[1]
    padded = -(-per * slots // 8) * 8 // slots
    dirs_per_tile = 1
    while dirs_per_tile * nears * per % 16:
        dirs_per_tile *= 2
    rows = dirs_per_tile * nears * per
    message = (slots * padded // 8, 8, channels)
    exchange = pltpu.VMEM((devices,) + message, BF16)
    any_spec = pl.BlockSpec(memory_space=pl.ANY)
    smem_spec = pl.BlockSpec(memory_space=pltpu.SMEM)
    return pl.pallas_call(
        functools.partial(kernel, (dirs, nears, per, padded, slots, dirs_per_tile)),
        out_shape=jax.ShapeDtypeStruct(currents.shape, BF16),
        in_specs=[smem_spec] * 3 + [any_spec] * 5,
        out_specs=pl.BlockSpec(memory_space=pltpu.VMEM),
        scratch_shapes=[
            pltpu.VMEM(currents.shape, BF16),
            pltpu.VMEM((slots * 8, unknowns, channels), BF16),
            pltpu.VMEM((3 * leaf_slots, unknowns, channels), BF16),
            pltpu.VMEM(near_blocks.shape, BF16),
            pltpu.VMEM(aggregate.shape, BF16),
            pltpu.VMEM(receive.shape, BF16),
            pltpu.VMEM(translations.shape, BF16),
            pltpu.VMEM((8 * unknowns, slots * channels), BF16),
            pltpu.VMEM((slots, rows, channels), F32),
            pltpu.VMEM((dirs_per_tile * nears * slots * padded, channels), F32),
            exchange,
            exchange,
            pltpu.VMEM((blocks, block_size * padded, channels), F32),
            pltpu.VMEM((blocks, block_size * padded, channels), F32),
            exchange,
            exchange,
            pltpu.VMEM((devices * slots * padded, channels), F32),
            pltpu.VMEM((directions, slots * channels), F32),
            pltpu.VMEM((directions, slots * channels), BF16),
            pltpu.VMEM((8, slots, unknowns, channels), F32),
            pltpu.VMEM((8, slots, unknowns, channels), BF16),
            pltpu.VMEM((8, slots, unknowns, channels), BF16),
            pltpu.VMEM((leaf_slots, unknowns, channels), F32),
            pltpu.SemaphoreType.DMA((6,)),
            pltpu.SemaphoreType.DMA((2,)),
            pltpu.SemaphoreType.DMA((2, 2)),
            pltpu.SemaphoreType.DMA((2, 2)),
            pltpu.SemaphoreType.DMA((2, 8)),
        ],
        compiler_params=pltpu.CompilerParams(
            collective_id=0, has_side_effects=True, vmem_limit_bytes=60 * 2**20
        ),
    )(
        counts,
        near_source.T,
        source_blocks,
        currents,
        near_blocks,
        aggregate,
        receive,
        translations,
    )


def solution(mesh):
    return jax.shard_map(
        body,
        mesh=mesh,
        in_specs=(
            P(("dir", "near"), None, None),
            P(),
            P(("dir", "near"), None),
            P(("dir", "near"), None, None, None),
            P(),
            P(),
            P(None, None, ("dir", "near"), None, None),
            P(),
        ),
        out_specs=P(("dir", "near"), None, None),
        check_vma=False,
    )
```

profile of v0, /device:TPU:0, one launch (start us, length us, event | category | flops | bytes accessed | tf_op | source)
XLA Modules:
  0.0 51.2 jit_solution(12416340747502080272)
XLA Ops:
  0.7 48.2 %shard_map.82 = bf16[32,128,128]{2,1,0:T(8,128)(2,1)} custom-call(s32[32]{0:T(128)} %counts.1, s32[6,32]{1,0:T(8,128)} %bitcast.1, s32[1,1]{1,0:T(1,128)S(6)} %copy.10.source_blocks, bf16[32,128,128]{2,1,0:T(8,128)(2,1)} %currents.1, bf16[32,6,128,256]{3,2,1,0:T(8,128)(2,1)} %near_blocks.1, bf16[8,1152,256]{2,1,0:T(8,128)(2,1)} %aggregate.1, ...), custom_call_target="tpu_custom_call" | custom-call | tf_op jit(solution)/shard_map/pallas_call | solution.py:370
  48.9 2.3 %copy.11 = bf16[32,128,128]{2,1,0:T(8,128)(2,1)} copy(bf16[32,128,128]{2,1,0:T(8,128)(2,1)} %shard_map.82) | data formatting | bytes 2097152
where the time goes:
time: 51.4 us; the launch traced here: 51.2 us
  Pallas kernels  48.2 us (94%)
  local copies, waits for them, and re-layouts  2.31 us (4%)
  between operations  0.66 us (1%)
    pallas_call x1, Pallas kernels, body(): pl.pallas_call(functools.partial(kernel, (dirs, nears, per, padded, slots...  48.2 us
    unnamed x1, local copies, waits for them, and re-layouts  2.31 us

commit v1 on v0

v1 whole, which is shorter than its diff:
```python
import functools

import jax
import jax.numpy as jnp
from jax import lax
from jax.experimental import pallas as pl
from jax.experimental.pallas import tpu as pltpu
from jax.sharding import PartitionSpec as P

MESH = pl.DeviceIdType.MESH
F32 = jnp.float32
BF16 = jnp.bfloat16
CHILDREN = 8


def turned(values):
    width = values.shape[-1]
    rolled = pltpu.roll(values, width // 2, values.ndim - 1)
    lane = lax.broadcasted_iota(jnp.int32, values.shape, values.ndim - 1)
    return jnp.where(lane < width // 2, -rolled, rolled)


def flipped(index, step, count):
    total = 0
    bit = 1
    while bit < count:
        total = total + bit * lax.rem(index // bit + step // bit, 2)
        bit *= 2
    return total


def chunks_of(per, slots):
    pieces = max(1, min(3, per // 4))
    base = per if pieces == 1 else per // pieces // 4 * 4
    sizes = [base] * (pieces - 1)
    sizes.append(per - sum(sizes))
    out, first = [], 0
    for size in sizes:
        out.append((first, size, -(-size * slots // 8) * 8 // slots))
        first += size
    return tuple(out)


def kernel(dims, counts, near_source, source_blocks, currents, near_blocks, aggregate, receive, translations, out, *scratch):
    dirs, nears, per, slots, chunks, tiles = dims
    devices = dirs * nears
    pieces = len(chunks)
    (
        pool,
        window,
        near_v,
        agg_v,
        rec_v,
        tra_v,
        stack,
        tile_rows,
        joined,
        fields,
        rec_last,
        fields_last,
        far_acc,
        far_own,
        far_send,
        far_recv,
        near_acc,
        load_sem,
        pair_sem,
        halo_sem,
        a2a_sem,
        far_sem,
    ) = scratch[:22]
    rest = scratch[22:]
    packs, send1, recv1, gathered, incoming, send2, recv2, spread = (
        rest[i * pieces : (i + 1) * pieces] for i in range(8)
    )
    leaf_slots, unknowns, channels = out.shape
    parent_slots = leaf_slots // CHILDREN
    half = parent_slots // 2
    near_per = near_v.shape[1]
    directions = agg_v.shape[1]
    dir_index = lax.axis_index("dir")
    near_index = lax.axis_index("near")
    me = dir_index * nears + near_index
    odd = lax.rem(near_index, 2)
    mate = near_index + 1 - 2 * odd
    half_leaves = half * CHILDREN
    own = pool.at[pl.ds(0, leaf_slots)]
    borrowed = pool.at[pl.ds(leaf_slots, half_leaves)]

    def deltas(index, count):
        steps, bit = [], 1
        while bit < count:
            steps.append((bit, bit - 2 * bit * lax.rem(index // bit, 2)))
            bit *= 2
        return steps

    dir_deltas, near_deltas = deltas(dir_index, dirs), deltas(near_index, nears)

    def partner(step):
        d, n = dir_index, near_index
        for bit, delta in dir_deltas:
            if step // nears & bit:
                d = d + delta
        for bit, delta in near_deltas:
            if step % nears & bit:
                n = n + delta
        return d, n

    load_own = pltpu.make_async_copy(currents, own, load_sem.at[0])
    load_agg = pltpu.make_async_copy(aggregate, agg_v, load_sem.at[1])
    load_mid = pltpu.make_async_copy(currents, window.at[pl.ds(leaf_slots, leaf_slots)], load_sem.at[2])
    load_tra = pltpu.make_async_copy(translations, tra_v, load_sem.at[3])
    load_rec = pltpu.make_async_copy(receive, rec_v, load_sem.at[4])
    load_near = pltpu.make_async_copy(near_blocks, near_v, load_sem.at[5])

    def start_pieces(source, target, sem, count):
        size = target.shape[0] // count
        for piece in range(count):
            cut = pl.ds(piece * size, size)
            pltpu.make_async_copy(source.at[cut], target.at[cut], sem).start()

    load_own.start()
    start_pieces(aggregate, agg_v, load_sem.at[1], 8)
    load_tra.start()
    start_pieces(receive, rec_v, load_sem.at[4], 8)
    load_mid.start()
    start_pieces(near_blocks, near_v, load_sem.at[5], 8)

    barrier = pltpu.get_barrier_semaphore()
    for step in range(1, devices):
        pl.semaphore_signal(barrier, inc=1, device_id=partner(step), device_id_type=MESH)
    pl.semaphore_wait(barrier, devices - 1)

    to_mate = pltpu.make_async_remote_copy(
        src_ref=currents.at[pl.ds((1 - odd) * half_leaves, half_leaves)],
        dst_ref=borrowed,
        send_sem=pair_sem.at[0],
        recv_sem=pair_sem.at[1],
        device_id=(dir_index, mate),
        device_id_type=MESH,
    )
    to_mate.start()

    own_count = counts[me]
    mate_count = counts[dir_index * nears + mate]
    even_count = jnp.where(odd == 0, own_count, mate_count)
    load_own.wait()
    to_mate.wait_recv()
    for w in range(half):
        is_own = jnp.where(odd == 0, w < own_count, half + w >= even_count)
        own_slot = jnp.clip(jnp.where(odd == 0, w, half + w - even_count), 0, parent_slots - 1)
        mate_slot = jnp.clip(jnp.where(odd == 0, w - own_count, w), 0, half - 1)
        slot = jnp.where(is_own, own_slot, parent_slots + mate_slot)
        for c in range(CHILDREN):
            values = pool[slot * CHILDREN + c]
            lanes = pl.ds(w * channels, channels)
            stack[pl.ds(2 * c * unknowns, unknowns), lanes] = values
            stack[pl.ds((2 * c + 1) * unknowns, unknowns), lanes] = turned(values.astype(F32)).astype(BF16)
    load_agg.wait()

    def hop(buffer, target, index, to, phase, p):
        return pltpu.make_async_remote_copy(
            src_ref=buffer.at[index],
            dst_ref=target.at[me],
            send_sem=a2a_sem.at[phase, p, 0],
            recv_sem=a2a_sem.at[phase, p, 1],
            device_id=to,
            device_id_type=MESH,
        )

    def all_moved(buffer, phase, p, which):
        some = buffer.at[pl.ds(0, devices - 1)]
        pltpu.make_async_copy(some, some, a2a_sem.at[phase, p, which]).wait()

    tile_devices = devices // tiles
    tile_dirs = tile_devices // nears
    rows = tile_devices * per
    my_tile = dir_index // tile_dirs

    def radiate(tile):
        start = pl.multiple_of(tile * rows, 16)
        left = jnp.concatenate([agg_v[c, pl.ds(start, rows), :] for c in range(CHILDREN)], axis=1)
        result = jnp.dot(left, stack[...], preferred_element_type=F32)
        for s in range(slots):
            tile_rows[s] = result[:, s * channels : (s + 1) * channels]

    def pack(tile, p):
        first, size, padded = chunks[p]
        for q in range(tile_devices):
            for s in range(slots):
                packs[p][pl.ds((q * slots + s) * padded, size), :] = tile_rows[s, pl.ds(q * per + first, size), :]
        shape = (tile_devices,) + send1[p].shape[1:]
        send1[p][pl.ds(tile * tile_devices, tile_devices)] = packs[p][...].reshape(shape).astype(BF16)

    def radiate_and_send(step, carry):
        tile = flipped(my_tile, tiles - 1 - step, tiles)
        radiate(tile)
        pack(tile, 0)
        for q in range(tile_devices):
            d, n = partner(q)
            d = d + (tile - my_tile) * tile_dirs
            hop(send1[0], recv1[0], d * nears + n, (d, n), 0, 0).start()
        for p in range(1, pieces):
            pack(tile, p)
        return carry

    lax.fori_loop(0, tiles - 1, radiate_and_send, 0)
    radiate(my_tile)
    pack(my_tile, 0)
    for q in range(1, tile_devices):
        d, n = partner(q)
        hop(send1[0], recv1[0], d * nears + n, (d, n), 0, 0).start()
    for p in range(1, pieces):
        pack(my_tile, p)
        for step in range(devices - 1, 0, -1):
            d, n = partner(step)
            hop(send1[p], recv1[p], d * nears + n, (d, n), 0, p).start()

    def halo(side, block):
        return pltpu.make_async_remote_copy(
            src_ref=currents,
            dst_ref=window.at[pl.ds(block * leaf_slots, leaf_slots)],
            send_sem=halo_sem.at[0, block // 2],
            recv_sem=halo_sem.at[1, block // 2],
            device_id=(dir_index, near_index + side),
            device_id_type=MESH,
        )

    @pl.when(near_index < nears - 1)
    def _():
        halo(1, 0).start()

    @pl.when(near_index > 0)
    def _():
        halo(-1, 2).start()

    for p in range(pieces):
        recv1[p][me] = send1[p][me]
    joined[...] = jnp.zeros_like(joined)

    load_rec.wait()
    last_first, last_size, _ = chunks[-1]
    last_total = devices * last_size
    for o in range(last_total // 128):
        ends = [(i // last_size) * per + last_first + i % last_size for i in (o * 128, o * 128 + 127)]
        low, high = ends[0] // 128 * 128, (ends[1] // 128 + 1) * 128
        row = lax.broadcasted_iota(jnp.int32, (high - low, 128), 0) + low
        column = lax.broadcasted_iota(jnp.int32, (high - low, 128), 1) + o * 128
        owner = (row * (2**16 // per + 1)) >> 16
        place = row - owner * per - last_first
        chosen = (place >= 0) & (place < last_size) & (owner * last_size + place == column)
        chooser = jnp.where(chosen, 1.0, 0.0).astype(BF16)
        for part in range(2):
            left = rec_v[:, :, pl.ds(part * directions + low, high - low)].reshape(CHILDREN * unknowns, high - low)
            picked = jnp.dot(left, chooser, preferred_element_type=F32).astype(BF16)
            rec_last[:, pl.ds(part * last_total + o * 128, 128)] = picked

    load_tra.wait()
    blocks, listed, _, block_size, doubled = tra_v.shape
    per_block = devices // blocks
    for p in range(pieces):
        first, size, padded = chunks[p]
        message = send1[p].shape[1:]
        all_moved(recv1[p], 0, p, 1)
        for b in range(blocks):
            got = recv1[p][pl.ds(b * per_block, per_block)].astype(F32)
            gathered[p][b] = got.reshape(gathered[p].shape[1:])
        for k in range(size):
            for b in range(blocks):
                summed = None
                for l in range(listed):
                    source = 0 if blocks == 1 else source_blocks[b, l]
                    rows_k = gathered[p][source, pl.ds(k, block_size, stride=padded), :]
                    both = jnp.concatenate([rows_k, turned(rows_k)], axis=0).astype(BF16)
                    part = jnp.dot(tra_v[b, l, first + k], both, preferred_element_type=F32)
                    summed = part if summed is None else summed + part
                incoming[p][b, pl.ds(k, block_size, stride=padded), :] = summed
        for b in range(blocks):
            packed = incoming[p][b].reshape((per_block,) + message)
            send2[p][pl.ds(b * per_block, per_block)] = packed.astype(BF16)
        for step in range(devices - 1, 0, -1):
            d, n = partner(step)
            hop(send2[p], recv2[p], d * nears + n, (d, n), 1, p).start()
        recv2[p][me] = send2[p][me]

    load_mid.wait()
    load_near.wait()

    @pl.when(near_index > 0)
    def _():
        halo(1, 0).wait_recv()

    @pl.when(near_index < nears - 1)
    def _():
        halo(-1, 2).wait_recv()

    base = (me - 1) * leaf_slots
    together = 4 if leaf_slots % 4 == 0 else 1

    def nearby(step, carry):
        for u in range(together):
            i = step * together + u
            rows_at = [near_source[e, i] - base for e in range(near_per)]
            sources = [window[jnp.clip(r, 0, 3 * leaf_slots - 1)] for r in rows_at]
            parts = [near_v[i, e] for e in range(near_per)]
            real = jnp.concatenate([p[:, :unknowns] for p in parts], axis=1)
            imag = jnp.concatenate([p[:, unknowns:] for p in parts], axis=1)
            result = jnp.dot(
                jnp.concatenate([real, imag], axis=0),
                jnp.concatenate(sources, axis=0),
                preferred_element_type=F32,
            )
            near_acc[i] = result[:unknowns] + turned(result[unknowns:])
        return carry

    lax.fori_loop(0, leaf_slots // together, nearby, 0)

    for p in range(pieces - 1):
        first, size, padded = chunks[p]
        all_moved(recv2[p], 1, p, 1)
        spread[p][...] = recv2[p][...].astype(F32).reshape(spread[p].shape)
        for d in range(devices):
            for s in range(slots):
                joined[s, pl.ds(d * per + first, size), :] = spread[p][pl.ds((d * slots + s) * padded, size), :]

    def fill(target, source, total):
        for s in range(slots):
            lanes = pl.ds(s * channels, channels)
            values = source[s]
            target[pl.ds(0, total), lanes] = values.astype(BF16)
            target[pl.ds(total, total), lanes] = turned(values).astype(BF16)

    group = 2

    if pieces > 1:
        fill(fields, joined, directions)

        def absorb_most(step, carry):
            left = rec_v[pl.ds(step * group, group)].reshape(group * unknowns, 2 * directions)
            start = pl.multiple_of(step * group * unknowns, group * unknowns)
            far_acc[pl.ds(start, group * unknowns), :] = jnp.dot(left, fields[...], preferred_element_type=F32)
            return carry

        lax.fori_loop(0, CHILDREN // group, absorb_most, 0)
    else:
        far_acc[...] = jnp.zeros_like(far_acc)

    p = pieces - 1
    first, size, padded = chunks[p]
    all_moved(recv2[p], 1, p, 1)
    spread[p][...] = recv2[p][...].astype(F32).reshape(spread[p].shape)
    for d in range(devices):
        for s in range(slots):
            joined[s, pl.ds(d * size, size), :] = spread[p][pl.ds((d * slots + s) * padded, size), :]
    fill(fields_last, joined.at[:, pl.ds(0, last_total)], last_total)

    def far_copy(c):
        return pltpu.make_async_remote_copy(
            src_ref=far_send.at[c],
            dst_ref=far_recv.at[c],
            send_sem=far_sem.at[0, c],
            recv_sem=far_sem.at[1, c],
            device_id=(dir_index, mate),
            device_id_type=MESH,
        )

    def absorb(step, carry):
        start = pl.multiple_of(step * group * unknowns, group * unknowns)
        far = far_acc[pl.ds(start, group * unknowns), :] + jnp.dot(
            rec_last[pl.ds(start, group * unknowns), :], fields_last[...], preferred_element_type=F32
        )
        for u in range(group):
            c = step * group + u
            for s in range(slots):
                piece = far[u * unknowns : (u + 1) * unknowns, s * channels : (s + 1) * channels]
                far_own[c, s] = piece
                far_send[c, s] = piece.astype(BF16)
            far_copy(c).start()
        return carry

    lax.fori_loop(0, CHILDREN // group, absorb, 0)

    def finish(c, carry):
        far_copy(c).wait_recv()
        for s in range(parent_slots):
            place = jnp.where(odd == 0, s, even_count + s)
            mine_at = place - half * odd
            mine = (mine_at >= 0) & (mine_at < half)
            own_at = jnp.clip(mine_at, 0, half - 1)
            mate_at = jnp.clip(place - half * (1 - odd), 0, half - 1)
            theirs = far_recv[c, 0]
            for w in range(1, half):
                theirs = jnp.where(mate_at == w, far_recv[c, w], theirs)
            far = jnp.where(mine, far_own[c, own_at], theirs.astype(F32))
            total = far + near_acc[s * CHILDREN + c]
            out[s * CHILDREN + c] = jnp.where(s < own_count, total, 0.0).astype(BF16)
        return carry

    lax.fori_loop(0, CHILDREN, finish, 0)

    to_mate.wait_send()
    for p in range(pieces):
        all_moved(send1[p], 0, p, 0)
        all_moved(send2[p], 1, p, 0)
    for c in range(CHILDREN):
        far_copy(c).wait_send()

    @pl.when(near_index < nears - 1)
    def _():
        halo(1, 0).wait_send()

    @pl.when(near_index > 0)
    def _():
        halo(-1, 2).wait_send()


def body(
    currents, counts, near_source, near_blocks, aggregate, receive, translations, source_blocks
):
    dirs, nears = lax.axis_size("dir"), lax.axis_size("near")
    devices = dirs * nears
    leaf_slots, unknowns, channels = currents.shape
    parent_slots = leaf_slots // CHILDREN
    slots = parent_slots // 2
    blocks, listed, per, block_size, doubled = translations.shape
    directions = aggregate.shape[1]
    chunks = chunks_of(per, slots)
    tiles = 4 if dirs % 4 == 0 and directions % 64 == 0 else 1
    tile_devices = devices // tiles
    lanes = slots * channels
    last_total = devices * chunks[-1][1]
    hbm_spec = pl.BlockSpec(memory_space=pltpu.HBM)
    smem_spec = pl.BlockSpec(memory_space=pltpu.SMEM)
    messages = [(devices, slots * padded // 8, 8, channels) for _, _, padded in chunks]
    exchange = [pltpu.VMEM(m, BF16) for m in messages]
    boxes = [pltpu.VMEM((blocks, block_size * padded, channels), F32) for _, _, padded in chunks]
    scratch = [
        pltpu.VMEM((leaf_slots + slots * CHILDREN, unknowns, channels), BF16),
        pltpu.VMEM((3 * leaf_slots, unknowns, channels), BF16),
        pltpu.VMEM(near_blocks.shape, BF16),
        pltpu.VMEM(aggregate.shape, BF16),
        pltpu.VMEM(receive.shape, BF16),
        pltpu.VMEM(translations.shape, BF16),
        pltpu.VMEM((2 * CHILDREN * unknowns, lanes), BF16),
        pltpu.VMEM((slots, tile_devices * per, channels), F32),
        pltpu.VMEM((slots, directions, channels), F32),
        pltpu.VMEM((2 * directions, lanes), BF16),
        pltpu.VMEM((CHILDREN * unknowns, 2 * last_total), BF16),
        pltpu.VMEM((2 * last_total, lanes), BF16),
        pltpu.VMEM((CHILDREN * unknowns, lanes), F32),
        pltpu.VMEM((CHILDREN, slots, unknowns, channels), F32),
        pltpu.VMEM((CHILDREN, slots, unknowns, channels), BF16),
        pltpu.VMEM((CHILDREN, slots, unknowns, channels), BF16),
        pltpu.VMEM((leaf_slots, unknowns, channels), F32),
        pltpu.SemaphoreType.DMA((6,)),
        pltpu.SemaphoreType.DMA((2,)),
        pltpu.SemaphoreType.DMA((2, 2)),
        pltpu.SemaphoreType.DMA((2, len(chunks), 2)),
        pltpu.SemaphoreType.DMA((2, CHILDREN)),
    ]
    scratch += [pltpu.VMEM((tile_devices * slots * padded, channels), F32) for _, _, padded in chunks]
    scratch += exchange + exchange + boxes + boxes + exchange + exchange
    scratch += [pltpu.VMEM((devices * slots * padded, channels), F32) for _, _, padded in chunks]
    return pl.pallas_call(
        functools.partial(kernel, (dirs, nears, per, slots, chunks, tiles)),
        out_shape=jax.ShapeDtypeStruct(currents.shape, BF16),
        in_specs=[smem_spec] * 3 + [hbm_spec] * 5,
        out_specs=pl.BlockSpec(memory_space=pltpu.VMEM),
        scratch_shapes=scratch,
        compiler_params=pltpu.CompilerParams(
            collective_id=0, has_side_effects=True, vmem_limit_bytes=50 * 2**20
        ),
    )(
        counts,
        near_source.T,
        source_blocks,
        currents,
        near_blocks,
        aggregate,
        receive,
        translations,
    )


def solution(mesh):
    return jax.shard_map(
        body,
        mesh=mesh,
        in_specs=(
            P(("dir", "near"), None, None),
            P(),
            P(("dir", "near"), None),
            P(("dir", "near"), None, None, None),
            P(),
            P(),
            P(None, None, ("dir", "near"), None, None),
            P(),
        ),
        out_specs=P(("dir", "near"), None, None),
        check_vma=False,
    )
```

time: 51.4 us -> 51.4 us (level)
  Pallas kernels: 48.2 us -> 45.9 us
  local copies, waits for them, and re-layouts: 2.31 us -> 4.6 us
    pallas_call x1, Pallas kernels: 48.2 us -> 45.9 us  [body(): pl.pallas_call(functools.partial(kernel, (dirs, nears, per, slots, chunks...]
    unnamed x1 -> x9, local copies, waits for them, and re-layouts: 2.31 us -> 4.6 us
where the time goes in v1:
time: 51.4 us; the launch traced here: 51.2 us
  Pallas kernels  45.9 us (89%)
  local copies, waits for them, and re-layouts  4.6 us (9%)
  between operations  0.67 us (1%)
    pallas_call x1, Pallas kernels, body(): pl.pallas_call(functools.partial(kernel, (dirs, nears, per, slots, chunks...  45.9 us
    unnamed x9, local copies, waits for them, and re-layouts  4.6 us

profile of v1, /device:TPU:0, one launch (start us, length us, event | category | flops | bytes accessed | tf_op | source)
XLA Modules:
  0.0 51.2 jit_solution(11680612829918068330)
XLA Ops:
  0.7 0.0 copy-start
  0.7 1.2 %copy-done = bf16[32,128,128]{2,1,0:T(8,128)(2,1)S(1)} copy-done((bf16[32,128,128]{2,1,0:T(8,128)(2,1)S(1)}, bf16[32,128,128]{2,1,0:T(8,128)(2,1)}, u32[]{:S(2)}) %copy-start) | copy-done | bytes 1048600
  1.9 0.0 copy-start.1
  1.9 1.1 %copy-done.1 = bf16[1,1,36,64,128]{4,3,2,1,0:T(8,128)(2,1)S(1)} copy-done((bf16[1,1,36,64,128]{4,3,2,1,0:T(8,128)(2,1)S(1)}, bf16[1,1,36,64,128]{4,3,2,1,0:T(8,128)(2,1)}, u32[]{:S(2)}) %copy-start.1) | copy-done | bytes 589848
  2.9 0.0 copy-start.2
  2.9 0.7 %copy-done.2 = s32[32,6]{0,1:T(8,128)S(1)} copy-done((s32[32,6]{0,1:T(8,128)S(1)}, s32[32,6]{0,1:T(8,128)}, u32[]{:S(2)}) %copy-start.2) | copy-done | bytes 792
  3.6 0.0 copy-start.3
  3.6 0.7 %copy-done.3 = s32[32]{0:T(128)S(1)} copy-done((s32[32]{0:T(128)S(1)}, s32[32]{0:T(128)}, u32[]{:S(2)}) %copy-start.3) | copy-done | bytes 152
  4.3 45.9 %shard_map.82 = bf16[32,128,128]{2,1,0:T(8,128)(2,1)S(1)} custom-call(s32[32]{0:T(128)S(1)} %copy-done.3, s32[6,32]{1,0:T(8,128)S(1)} %bitcast.1, s32[1,1]{1,0:T(1,128)S(6)} %copy.10.source_blocks, bf16[32,128,128]{2,1,0:T(8,128)(2,1)S(1)} %copy-done, bf16[32,6,128,256]{3,2,1,0:T(8,128)(2,1)} %near_blocks.1, bf16[8,1152,256]{2,1,0:T(8,128)(2,1)} %aggregate.1, ...), custom_call_target="tpu_custom_call" | custom-call | tf_op jit(solution)/shard_map/pallas_call | solution.py:464
  50.2 1.0 %copy.11 = bf16[32,128,128]{2,1,0:T(8,128)(2,1)} copy(bf16[32,128,128]{2,1,0:T(8,128)(2,1)S(1)} %shard_map.82) | data formatting | bytes 2097152
Async XLA Ops:
  0.7 1.2 %copy-start = (bf16[32,128,128]{2,1,0:T(8,128)(2,1)S(1)}, bf16[32,128,128]{2,1,0:T(8,128)(2,1)}, u32[]{:S(2)}) copy-start(bf16[32,128,128]{2,1,0:T(8,128)(2,1)} %currents.1) | copy-start | bytes 3145732
  1.9 1.1 %copy-start.1 = (bf16[1,1,36,64,128]{4,3,2,1,0:T(8,128)(2,1)S(1)}, bf16[1,1,36,64,128]{4,3,2,1,0:T(8,128)(2,1)}, u32[]{:S(2)}) copy-start(bf16[1,1,36,64,128]{4,3,2,1,0:T(8,128)(2,1)} %translations.1) | copy-start | bytes 1769476
  2.9 0.7 %copy-start.2 = (s32[32,6]{0,1:T(8,128)S(1)}, s32[32,6]{0,1:T(8,128)}, u32[]{:S(2)}) copy-start(s32[32,6]{0,1:T(8,128)} %param.10) | copy-start | bytes 2308
  3.6 0.7 %copy-start.3 = (s32[32]{0:T(128)S(1)}, s32[32]{0:T(128)}, u32[]{:S(2)}) copy-start(s32[32]{0:T(128)} %counts.1) | copy-start | bytes 388

commit v2 on v1

--- a/solution.py
+++ b/solution.py
@@ -29,10 +29,13 @@
     return total
 
 
+SHARES = (12, 12, 12)
+HALO = (4, 6, 6)
+
+
 def chunks_of(per, slots):
-    pieces = max(1, min(3, per // 4))
-    base = per if pieces == 1 else per // pieces // 4 * 4
-    sizes = [base] * (pieces - 1)
+    sizes = [per * share // sum(SHARES) // 4 * 4 for share in SHARES[:-1]]
+    sizes = [size for size in sizes if size]
     sizes.append(per - sum(sizes))
     out, first = [], 0
     for size in sizes:
@@ -41,10 +44,19 @@
     return tuple(out)
 
 
-def kernel(dims, counts, near_source, source_blocks, currents, near_blocks, aggregate, receive, translations, out, *scratch):
-    dirs, nears, per, slots, chunks, tiles = dims
+def halo_parts_of(leaf_slots, pieces):
+    sizes = [HALO[i] * leaf_slots // 32 if i < len(HALO) else 0 for i in range(pieces)]
+    sizes.append(leaf_slots - sum(sizes))
+    return tuple((sum(sizes[:i]), size) for i, size in enumerate(sizes))
+
+
+def kernel(dims, *refs):
+    dirs, nears, per, slots, chunks, halo_parts, tiles, listing = dims
     devices = dirs * nears
     pieces = len(chunks)
+    source_blocks, refs = (refs[0], refs[1:]) if listing else (None, refs)
+    counts_hbm, near_source_hbm, currents, near_blocks, aggregate, receive, translations, out = refs[:8]
+    scratch = refs[8:]
     (
         pool,
         window,
@@ -64,12 +76,17 @@
         far_recv,
         near_acc,
         load_sem,
+        agg_sem,
         pair_sem,
         halo_sem,
         a2a_sem,
         far_sem,
-    ) = scratch[:22]
-    rest = scratch[22:]
+        met_sem,
+        counts,
+        near_source,
+        small_sem,
+    ) = scratch[:27]
+    rest = scratch[27:]
     packs, send1, recv1, gathered, incoming, send2, recv2, spread = (
         rest[i * pieces : (i + 1) * pieces] for i in range(8)
     )
@@ -107,7 +124,7 @@
         return d, n
 
     load_own = pltpu.make_async_copy(currents, own, load_sem.at[0])
-    load_agg = pltpu.make_async_copy(aggregate, agg_v, load_sem.at[1])
+    load_source = pltpu.make_async_copy(near_source_hbm, near_source, small_sem.at[1])
     load_mid = pltpu.make_async_copy(currents, window.at[pl.ds(leaf_slots, leaf_slots)], load_sem.at[2])
     load_tra = pltpu.make_async_copy(translations, tra_v, load_sem.at[3])
     load_rec = pltpu.make_async_copy(receive, rec_v, load_sem.at[4])
@@ -119,17 +136,40 @@
             cut = pl.ds(piece * size, size)
             pltpu.make_async_copy(source.at[cut], target.at[cut], sem).start()
 
+    tile_devices = devices // tiles
+    tile_dirs = tile_devices // nears
+    rows = tile_devices * per
+    my_tile = dir_index // tile_dirs
+
+    def load_rows(step):
+        tile = flipped(my_tile, tiles - 1 - step, tiles)
+        cut = pl.ds(pl.multiple_of(tile * rows, 16), rows)
+        return pltpu.make_async_copy(aggregate.at[:, cut, :], agg_v.at[:, cut, :], agg_sem.at[step])
+
+    load_counts = pltpu.make_async_copy(counts_hbm, counts, small_sem.at[0])
+    load_counts.start()
     load_own.start()
-    start_pieces(aggregate, agg_v, load_sem.at[1], 8)
+    for step in range(tiles):
+        load_rows(step).start()
     load_tra.start()
     start_pieces(receive, rec_v, load_sem.at[4], 8)
+    load_source.start()
     load_mid.start()
     start_pieces(near_blocks, near_v, load_sem.at[5], 8)
 
     barrier = pltpu.get_barrier_semaphore()
-    for step in range(1, devices):
-        pl.semaphore_signal(barrier, inc=1, device_id=partner(step), device_id_type=MESH)
-    pl.semaphore_wait(barrier, devices - 1)
+    @pl.when(odd == 0)
+    def _():
+        pl.semaphore_signal(barrier, inc=1, device_id=(dir_index, mate), device_id_type=MESH)
+
+    @pl.when(odd == 1)
+    def _():
+        pl.semaphore_wait(barrier, 1)
+        pl.semaphore_signal(met_sem, inc=1, device_id=(dir_index, mate), device_id_type=MESH)
+
+    @pl.when(odd == 0)
+    def _():
+        pl.semaphore_wait(met_sem, 1)
 
     to_mate = pltpu.make_async_remote_copy(
         src_ref=currents.at[pl.ds((1 - odd) * half_leaves, half_leaves)],
@@ -141,6 +181,12 @@
     )
     to_mate.start()
 
+    @pl.when(odd == 0)
+    def _():
+        for step in range(devices - 2, 0, -2):
+            pl.semaphore_signal(barrier, inc=1, device_id=partner(step), device_id_type=MESH)
+
+    load_counts.wait()
     own_count = counts[me]
     mate_count = counts[dir_index * nears + mate]
     even_count = jnp.where(odd == 0, own_count, mate_count)
@@ -156,7 +202,6 @@
             lanes = pl.ds(w * channels, channels)
             stack[pl.ds(2 * c * unknowns, unknowns), lanes] = values
             stack[pl.ds((2 * c + 1) * unknowns, unknowns), lanes] = turned(values.astype(F32)).astype(BF16)
-    load_agg.wait()
 
     def hop(buffer, target, index, to, phase, p):
         return pltpu.make_async_remote_copy(
@@ -172,11 +217,6 @@
         some = buffer.at[pl.ds(0, devices - 1)]
         pltpu.make_async_copy(some, some, a2a_sem.at[phase, p, which]).wait()
 
-    tile_devices = devices // tiles
-    tile_dirs = tile_devices // nears
-    rows = tile_devices * per
-    my_tile = dir_index // tile_dirs
-
     def radiate(tile):
         start = pl.multiple_of(tile * rows, 16)
         left = jnp.concatenate([agg_v[c, pl.ds(start, rows), :] for c in range(CHILDREN)], axis=1)
@@ -192,10 +232,51 @@
         shape = (tile_devices,) + send1[p].shape[1:]
         send1[p][pl.ds(tile * tile_devices, tile_devices)] = packs[p][...].reshape(shape).astype(BF16)
 
+    def all_here():
+        @pl.when(odd == 0)
+        def _():
+            pl.semaphore_wait(barrier, devices // 2 - 1)
+            pl.semaphore_signal(met_sem, inc=1, device_id=(dir_index, mate), device_id_type=MESH)
+
+        @pl.when(odd == 1)
+        def _():
+            pl.semaphore_wait(met_sem, 1)
+
+    def halo(side, block, first=0, size=None):
+        size = leaf_slots if size is None else size
+        return pltpu.make_async_remote_copy(
+            src_ref=currents.at[pl.ds(first, size)],
+            dst_ref=window.at[pl.ds(block * leaf_slots + first, size)],
+            send_sem=halo_sem.at[0, block // 2],
+            recv_sem=halo_sem.at[1, block // 2],
+            device_id=(dir_index, near_index + side),
+            device_id_type=MESH,
+        )
+
+    def start_halo(part):
+        first, size = halo_parts[part]
+        if size == 0:
+            return
+
+        @pl.when(near_index < nears - 1)
+        def _():
+            halo(1, 0, first, size).start()
+
+        @pl.when(near_index > 0)
+        def _():
+            halo(-1, 2, first, size).start()
+
     def radiate_and_send(step, carry):
         tile = flipped(my_tile, tiles - 1 - step, tiles)
+        load_rows(step).wait()
         radiate(tile)
         pack(tile, 0)
+
+        @pl.when(step == 0)
+        def _():
+            all_here()
+            start_halo(0)
+
         for q in range(tile_devices):
             d, n = partner(q)
             d = d + (tile - my_tile) * tile_dirs
@@ -205,34 +286,23 @@
         return carry
 
     lax.fori_loop(0, tiles - 1, radiate_and_send, 0)
+    load_rows(tiles - 1).wait()
     radiate(my_tile)
     pack(my_tile, 0)
+    if tiles == 1:
+        all_here()
+        start_halo(0)
     for q in range(1, tile_devices):
         d, n = partner(q)
         hop(send1[0], recv1[0], d * nears + n, (d, n), 0, 0).start()
     for p in range(1, pieces):
         pack(my_tile, p)
+        start_halo(p)
         for step in range(devices - 1, 0, -1):
             d, n = partner(step)
             hop(send1[p], recv1[p], d * nears + n, (d, n), 0, p).start()
 
-    def halo(side, block):
-        return pltpu.make_async_remote_copy(
-            src_ref=currents,
-            dst_ref=window.at[pl.ds(block * leaf_slots, leaf_slots)],
-            send_sem=halo_sem.at[0, block // 2],
-            recv_sem=halo_sem.at[1, block // 2],
-            device_id=(dir_index, near_index + side),
-            device_id_type=MESH,
-        )
-
-    @pl.when(near_index < nears - 1)
-    def _():
-        halo(1, 0).start()
-
-    @pl.when(near_index > 0)
-    def _():
-        halo(-1, 2).start()
+    start_halo(pieces)
 
     for p in range(pieces):
         recv1[p][me] = send1[p][me]
@@ -269,7 +339,7 @@
             for b in range(blocks):
                 summed = None
                 for l in range(listed):
-                    source = 0 if blocks == 1 else source_blocks[b, l]
+                    source = source_blocks[b, l] if listing else 0
                     rows_k = gathered[p][source, pl.ds(k, block_size, stride=padded), :]
                     both = jnp.concatenate([rows_k, turned(rows_k)], axis=0).astype(BF16)
                     part = jnp.dot(tra_v[b, l, first + k], both, preferred_element_type=F32)
@@ -285,6 +355,7 @@
 
     load_mid.wait()
     load_near.wait()
+    load_source.wait()
 
     @pl.when(near_index > 0)
     def _():
@@ -429,8 +500,8 @@
     tile_devices = devices // tiles
     lanes = slots * channels
     last_total = devices * chunks[-1][1]
+    listing = [source_blocks] if blocks > 1 else []
     hbm_spec = pl.BlockSpec(memory_space=pltpu.HBM)
-    smem_spec = pl.BlockSpec(memory_space=pltpu.SMEM)
     messages = [(devices, slots * padded // 8, 8, channels) for _, _, padded in chunks]
     exchange = [pltpu.VMEM(m, BF16) for m in messages]
     boxes = [pltpu.VMEM((blocks, block_size * padded, channels), F32) for _, _, padded in chunks]
@@ -453,32 +524,42 @@
         pltpu.VMEM((CHILDREN, slots, unknowns, channels), BF16),
         pltpu.VMEM((leaf_slots, unknowns, channels), F32),
         pltpu.SemaphoreType.DMA((6,)),
+        pltpu.SemaphoreType.DMA((tiles,)),
         pltpu.SemaphoreType.DMA((2,)),
         pltpu.SemaphoreType.DMA((2, 2)),
         pltpu.SemaphoreType.DMA((2, len(chunks), 2)),
         pltpu.SemaphoreType.DMA((2, CHILDREN)),
+        pltpu.SemaphoreType.REGULAR,
+        pltpu.SMEM((devices,), jnp.int32),
+        pltpu.SMEM((near_blocks.shape[1], leaf_slots), jnp.int32),
+        pltpu.SemaphoreType.DMA((2,)),
     ]
     scratch += [pltpu.VMEM((tile_devices * slots * padded, channels), F32) for _, _, padded in chunks]
     scratch += exchange + exchange + boxes + boxes + exchange + exchange
     scratch += [pltpu.VMEM((devices * slots * padded, channels), F32) for _, _, padded in chunks]
     return pl.pallas_call(
-        functools.partial(kernel, (dirs, nears, per, slots, chunks, tiles)),
+        functools.partial(kernel, (dirs, nears, per, slots, chunks, halo_parts_of(leaf_slots, len(chunks)), tiles, blocks > 1)),
         out_shape=jax.ShapeDtypeStruct(currents.shape, BF16),
-        in_specs=[smem_spec] * 3 + [hbm_spec] * 5,
+        in_specs=[pl.BlockSpec(memory_space=pltpu.SMEM)] * len(listing) + [hbm_spec] * 7,
         out_specs=pl.BlockSpec(memory_space=pltpu.VMEM),
         scratch_shapes=scratch,
         compiler_params=pltpu.CompilerParams(
             collective_id=0, has_side_effects=True, vmem_limit_bytes=50 * 2**20
         ),
     )(
-        counts,
-        near_source.T,
-        source_blocks,
-        currents,
-        near_blocks,
-        aggregate,
-        receive,
-        translations,
+        *listing,
+        *(
+            pltpu.with_memory_space_constraint(array, pltpu.HBM)
+            for array in (
+                counts,
+                near_source.T,
+                currents,
+                near_blocks,
+                aggregate,
+                receive,
+                translations,
+            )
+        ),
     )
 
 

time: 51.4 us -> 44.5 us (0.87)
  local copies, waits for them, and re-layouts: 4.6 us -> 0.97 us
  Pallas kernels: 45.9 us -> 43.4 us
  between operations: 0.67 us -> 0.01 us
    unnamed x9 -> x1, local copies, waits for them, and re-layouts: 4.6 us -> 0.97 us
    pallas_call x1, Pallas kernels: 45.9 us -> 43.4 us  [body(): pl.pallas_call(functools.partial(kernel, (dirs, nears, per, slots, chunks...]
where the time goes in v2:
time: 44.5 us; the launch traced here: 44.4 us
  Pallas kernels  43.4 us (98%)
  local copies, waits for them, and re-layouts  0.97 us (2%)
    pallas_call x1, Pallas kernels, body(): pl.pallas_call(functools.partial(kernel, (dirs, nears, per, slots, chunks...  43.4 us
    unnamed x1, local copies, waits for them, and re-layouts  0.97 us

profile of v2, /device:TPU:0, one launch (start us, length us, event | category | flops | bytes accessed | tf_op | source)
XLA Modules:
  0.0 44.4 jit_solution(14872927327337149719)
XLA Ops:
  0.0 43.4 %shard_map.73 = bf16[32,128,128]{2,1,0:T(8,128)(2,1)S(1)} custom-call(s32[32]{0:T(128)} %refs_0_.1, s32[6,32]{1,0:T(8,128)} %bitcast.1, bf16[32,128,128]{2,1,0:T(8,128)(2,1)} %refs_2_.1, bf16[32,6,128,256]{3,2,1,0:T(8,128)(2,1)} %refs_3_.1, bf16[8,1152,256]{2,1,0:T(8,128)(2,1)} %refs_4_.1, bf16[8,128,2304]{2,1,0:T(8,128)(2,1)} %refs_5_.1, ...), custom_call_target="tpu_custom_call" | custom-call | tf_op jit(solution)/shard_map/pallas_call | solution.py:540
  43.4 1.0 %copy.9 = bf16[32,128,128]{2,1,0:T(8,128)(2,1)} copy(bf16[32,128,128]{2,1,0:T(8,128)(2,1)S(1)} %shard_map.73) | data formatting | bytes 2097152

commit v3 on v2

--- a/solution.py
+++ b/solution.py
@@ -29,8 +29,8 @@
     return total
 
 
-SHARES = (12, 12, 12)
-HALO = (4, 6, 6)
+SHARES = (16, 12, 8)
+HALO = (8, 16, 8)
 
 
 def chunks_of(per, slots):
@@ -68,8 +68,7 @@
         tile_rows,
         joined,
         fields,
-        rec_last,
-        fields_last,
+        rec_sorted,
         far_acc,
         far_own,
         far_send,
@@ -85,8 +84,8 @@
         counts,
         near_source,
         small_sem,
-    ) = scratch[:27]
-    rest = scratch[27:]
+    ) = scratch[:26]
+    rest = scratch[26:]
     packs, send1, recv1, gathered, incoming, send2, recv2, spread = (
         rest[i * pieces : (i + 1) * pieces] for i in range(8)
     )
@@ -151,11 +150,6 @@
     load_own.start()
     for step in range(tiles):
         load_rows(step).start()
-    load_tra.start()
-    start_pieces(receive, rec_v, load_sem.at[4], 8)
-    load_source.start()
-    load_mid.start()
-    start_pieces(near_blocks, near_v, load_sem.at[5], 8)
 
     barrier = pltpu.get_barrier_semaphore()
     @pl.when(odd == 0)
@@ -287,6 +281,11 @@
 
     lax.fori_loop(0, tiles - 1, radiate_and_send, 0)
     load_rows(tiles - 1).wait()
+    load_tra.start()
+    load_source.start()
+    start_pieces(receive, rec_v, load_sem.at[4], 8)
+    load_mid.start()
+    start_pieces(near_blocks, near_v, load_sem.at[5], 8)
     radiate(my_tile)
     pack(my_tile, 0)
     if tiles == 1:
@@ -306,24 +305,23 @@
 
     for p in range(pieces):
         recv1[p][me] = send1[p][me]
-    joined[...] = jnp.zeros_like(joined)
 
     load_rec.wait()
-    last_first, last_size, _ = chunks[-1]
-    last_total = devices * last_size
-    for o in range(last_total // 128):
-        ends = [(i // last_size) * per + last_first + i % last_size for i in (o * 128, o * 128 + 127)]
-        low, high = ends[0] // 128 * 128, (ends[1] // 128 + 1) * 128
-        row = lax.broadcasted_iota(jnp.int32, (high - low, 128), 0) + low
-        column = lax.broadcasted_iota(jnp.int32, (high - low, 128), 1) + o * 128
-        owner = (row * (2**16 // per + 1)) >> 16
-        place = row - owner * per - last_first
-        chosen = (place >= 0) & (place < last_size) & (owner * last_size + place == column)
-        chooser = jnp.where(chosen, 1.0, 0.0).astype(BF16)
-        for part in range(2):
-            left = rec_v[:, :, pl.ds(part * directions + low, high - low)].reshape(CHILDREN * unknowns, high - low)
-            picked = jnp.dot(left, chooser, preferred_element_type=F32).astype(BF16)
-            rec_last[:, pl.ds(part * last_total + o * 128, 128)] = picked
+    for first, size, _ in chunks:
+        total, place = devices * size, 2 * devices * first
+        for o in range(total // 128):
+            ends = [(i // size) * per + first + i % size for i in (o * 128, o * 128 + 127)]
+            low, high = ends[0] // 128 * 128, (ends[1] // 128 + 1) * 128
+            row = lax.broadcasted_iota(jnp.int32, (high - low, 128), 0) + low
+            column = lax.broadcasted_iota(jnp.int32, (high - low, 128), 1) + o * 128
+            owner = (row * (2**16 // per + 1)) >> 16
+            inner = row - owner * per - first
+            chosen = (inner >= 0) & (inner < size) & (owner * size + inner == column)
+            chooser = jnp.where(chosen, 1.0, 0.0).astype(BF16)
+            for part in range(2):
+                left = rec_v[:, :, pl.ds(part * directions + low, high - low)].reshape(CHILDREN * unknowns, high - low)
+                picked = jnp.dot(left, chooser, preferred_element_type=F32).astype(BF16)
+                rec_sorted[:, pl.ds(place + part * total + o * 128, 128)] = picked
 
     load_tra.wait()
     blocks, listed, _, block_size, doubled = tra_v.shape
@@ -366,7 +364,7 @@
         halo(-1, 2).wait_recv()
 
     base = (me - 1) * leaf_slots
-    together = 4 if leaf_slots % 4 == 0 else 1
+    together = 8 if leaf_slots % 8 == 0 else 1
 
     def nearby(step, carry):
         for u in range(together):
@@ -386,44 +384,43 @@
 
     lax.fori_loop(0, leaf_slots // together, nearby, 0)
 
+    def unpack(p):
+        first, size, padded = chunks[p]
+        total, place = devices * size, 2 * devices * first
+        all_moved(recv2[p], 1, p, 1)
+        if size % 8:
+            spread[p][...] = recv2[p][...].astype(F32).reshape(spread[p].shape)
+        for s in range(slots):
+            if size % 8:
+                for d in range(devices):
+                    joined[pl.ds(d * size, size), :] = spread[p][pl.ds((d * slots + s) * padded, size), :]
+                values = joined[pl.ds(0, total), :]
+            else:
+                values = recv2[p][:, s * size // 8 : (s + 1) * size // 8].astype(F32).reshape(total, channels)
+            lanes = pl.ds(s * channels, channels)
+            fields[pl.ds(place, total), lanes] = values.astype(BF16)
+            fields[pl.ds(place + total, total), lanes] = turned(values).astype(BF16)
+
+    group = 2
+    height = group * unknowns
+    split = 2 * devices * chunks[-1][0]
+    rest_depth = 2 * directions - split
+
     for p in range(pieces - 1):
-        first, size, padded = chunks[p]
-        all_moved(recv2[p], 1, p, 1)
-        spread[p][...] = recv2[p][...].astype(F32).reshape(spread[p].shape)
-        for d in range(devices):
-            for s in range(slots):
-                joined[s, pl.ds(d * per + first, size), :] = spread[p][pl.ds((d * slots + s) * padded, size), :]
-
-    def fill(target, source, total):
-        for s in range(slots):
-            lanes = pl.ds(s * channels, channels)
-            values = source[s]
-            target[pl.ds(0, total), lanes] = values.astype(BF16)
-            target[pl.ds(total, total), lanes] = turned(values).astype(BF16)
-
-    group = 2
-
+        unpack(p)
     if pieces > 1:
-        fill(fields, joined, directions)
 
         def absorb_most(step, carry):
-            left = rec_v[pl.ds(step * group, group)].reshape(group * unknowns, 2 * directions)
-            start = pl.multiple_of(step * group * unknowns, group * unknowns)
-            far_acc[pl.ds(start, group * unknowns), :] = jnp.dot(left, fields[...], preferred_element_type=F32)
+            start = pl.multiple_of(step * height, height)
+            far_acc[pl.ds(start, height), :] = jnp.dot(
+                rec_sorted[pl.ds(start, height), pl.ds(0, split)],
+                fields[pl.ds(0, split), :],
+                preferred_element_type=F32,
+            )
             return carry
 
         lax.fori_loop(0, CHILDREN // group, absorb_most, 0)
-    else:
-        far_acc[...] = jnp.zeros_like(far_acc)
-
-    p = pieces - 1
-    first, size, padded = chunks[p]
-    all_moved(recv2[p], 1, p, 1)
-    spread[p][...] = recv2[p][...].astype(F32).reshape(spread[p].shape)
-    for d in range(devices):
-        for s in range(slots):
-            joined[s, pl.ds(d * size, size), :] = spread[p][pl.ds((d * slots + s) * padded, size), :]
-    fill(fields_last, joined.at[:, pl.ds(0, last_total)], last_total)
+    unpack(pieces - 1)
 
     def far_copy(c):
         return pltpu.make_async_remote_copy(
@@ -436,10 +433,14 @@
         )
 
     def absorb(step, carry):
-        start = pl.multiple_of(step * group * unknowns, group * unknowns)
-        far = far_acc[pl.ds(start, group * unknowns), :] + jnp.dot(
-            rec_last[pl.ds(start, group * unknowns), :], fields_last[...], preferred_element_type=F32
+        start = pl.multiple_of(step * height, height)
+        far = jnp.dot(
+            rec_sorted[pl.ds(start, height), pl.ds(split, rest_depth)],
+            fields[pl.ds(split, rest_depth), :],
+            preferred_element_type=F32,
         )
+        if pieces > 1:
+            far = far + far_acc[pl.ds(start, height), :]
         for u in range(group):
             c = step * group + u
             for s in range(slots):
@@ -499,7 +500,6 @@
     tiles = 4 if dirs % 4 == 0 and directions % 64 == 0 else 1
     tile_devices = devices // tiles
     lanes = slots * channels
-    last_total = devices * chunks[-1][1]
     listing = [source_blocks] if blocks > 1 else []
     hbm_spec = pl.BlockSpec(memory_space=pltpu.HBM)
     messages = [(devices, slots * padded // 8, 8, channels) for _, _, padded in chunks]
@@ -514,10 +514,9 @@
         pltpu.VMEM(translations.shape, BF16),
         pltpu.VMEM((2 * CHILDREN * unknowns, lanes), BF16),
         pltpu.VMEM((slots, tile_devices * per, channels), F32),
-        pltpu.VMEM((slots, directions, channels), F32),
+        pltpu.VMEM((devices * max(size for _, size, _ in chunks), channels), F32),
         pltpu.VMEM((2 * directions, lanes), BF16),
-        pltpu.VMEM((CHILDREN * unknowns, 2 * last_total), BF16),
-        pltpu.VMEM((2 * last_total, lanes), BF16),
+        pltpu.VMEM((CHILDREN * unknowns, 2 * directions), BF16),
         pltpu.VMEM((CHILDREN * unknowns, lanes), F32),
         pltpu.VMEM((CHILDREN, slots, unknowns, channels), F32),
         pltpu.VMEM((CHILDREN, slots, unknowns, channels), BF16),

time: 44.5 us -> 41 us (0.921)
  Pallas kernels: 43.4 us -> 39.9 us
    pallas_call x1, Pallas kernels: 43.4 us -> 39.9 us  [body(): pl.pallas_call(functools.partial(kernel, (dirs, nears, per, slots, chunks...]
where the time goes in v3:
time: 41 us; the launch traced here: 40.9 us
  Pallas kernels  39.9 us (97%)
  local copies, waits for them, and re-layouts  0.97 us (2%)
    pallas_call x1, Pallas kernels, body(): pl.pallas_call(functools.partial(kernel, (dirs, nears, per, slots, chunks...  39.9 us
    unnamed x1, local copies, waits for them, and re-layouts  0.97 us

profile of v3, /device:TPU:0, one launch (start us, length us, event | category | flops | bytes accessed | tf_op | source)
XLA Modules:
  0.0 40.9 jit_solution(16408037470567087819)
XLA Ops:
  0.0 39.9 %shard_map.73 = bf16[32,128,128]{2,1,0:T(8,128)(2,1)S(1)} custom-call(s32[32]{0:T(128)} %refs_0_.1, s32[6,32]{1,0:T(8,128)} %bitcast.1, bf16[32,128,128]{2,1,0:T(8,128)(2,1)} %refs_2_.1, bf16[32,6,128,256]{3,2,1,0:T(8,128)(2,1)} %refs_3_.1, bf16[8,1152,256]{2,1,0:T(8,128)(2,1)} %refs_4_.1, bf16[8,128,2304]{2,1,0:T(8,128)(2,1)} %refs_5_.1, ...), custom_call_target="tpu_custom_call" | custom-call | tf_op jit(solution)/shard_map/pallas_call | solution.py:539
  39.9 1.0 %copy.9 = bf16[32,128,128]{2,1,0:T(8,128)(2,1)} copy(bf16[32,128,128]{2,1,0:T(8,128)(2,1)S(1)} %shard_map.73) | data formatting | bytes 2097152

commit v4 on v3

--- a/solution.py
+++ b/solution.py
@@ -29,7 +29,7 @@
     return total
 
 
-SHARES = (16, 12, 8)
+SHARES = (12, 12, 12)
 HALO = (8, 16, 8)
 
 
@@ -122,6 +122,12 @@
                 n = n + delta
         return d, n
 
+    barrier = pltpu.get_barrier_semaphore()
+
+    @pl.when(odd == 0)
+    def _():
+        pl.semaphore_signal(barrier, inc=1, device_id=(dir_index, mate), device_id_type=MESH)
+
     load_own = pltpu.make_async_copy(currents, own, load_sem.at[0])
     load_source = pltpu.make_async_copy(near_source_hbm, near_source, small_sem.at[1])
     load_mid = pltpu.make_async_copy(currents, window.at[pl.ds(leaf_slots, leaf_slots)], load_sem.at[2])
@@ -150,11 +156,6 @@
     load_own.start()
     for step in range(tiles):
         load_rows(step).start()
-
-    barrier = pltpu.get_barrier_semaphore()
-    @pl.when(odd == 0)
-    def _():
-        pl.semaphore_signal(barrier, inc=1, device_id=(dir_index, mate), device_id_type=MESH)
 
     @pl.when(odd == 1)
     def _():
@@ -401,7 +402,7 @@
             fields[pl.ds(place, total), lanes] = values.astype(BF16)
             fields[pl.ds(place + total, total), lanes] = turned(values).astype(BF16)
 
-    group = 2
+    group = 4
     height = group * unknowns
     split = 2 * devices * chunks[-1][0]
     rest_depth = 2 * directions - split

time: 41 us -> 40.5 us (0.988)
  Pallas kernels: 39.9 us -> 39.4 us
    pallas_call x1, Pallas kernels: 39.9 us -> 39.4 us  [body(): pl.pallas_call(functools.partial(kernel, (dirs, nears, per, slots, chunks...]
where the time goes in v4:
time: 40.5 us; the launch traced here: 40.3 us
  Pallas kernels  39.4 us (97%)
  local copies, waits for them, and re-layouts  0.97 us (2%)
    pallas_call x1, Pallas kernels, body(): pl.pallas_call(functools.partial(kernel, (dirs, nears, per, slots, chunks...  39.4 us
    unnamed x1, local copies, waits for them, and re-layouts  0.97 us

profile of v4, /device:TPU:0, one launch (start us, length us, event | category | flops | bytes accessed | tf_op | source)
XLA Modules:
  0.0 40.3 jit_solution(2704694077405197265)
XLA Ops:
  0.0 39.4 %shard_map.73 = bf16[32,128,128]{2,1,0:T(8,128)(2,1)S(1)} custom-call(s32[32]{0:T(128)} %refs_0_.1, s32[6,32]{1,0:T(8,128)} %bitcast.1, bf16[32,128,128]{2,1,0:T(8,128)(2,1)} %refs_2_.1, bf16[32,6,128,256]{3,2,1,0:T(8,128)(2,1)} %refs_3_.1, bf16[8,1152,256]{2,1,0:T(8,128)(2,1)} %refs_4_.1, bf16[8,128,2304]{2,1,0:T(8,128)(2,1)} %refs_5_.1, ...), custom_call_target="tpu_custom_call" | custom-call | tf_op jit(solution)/shard_map/pallas_call | solution.py:540
  39.4 1.0 %copy.9 = bf16[32,128,128]{2,1,0:T(8,128)(2,1)} copy(bf16[32,128,128]{2,1,0:T(8,128)(2,1)S(1)} %shard_map.73) | data formatting | bytes 2097152

commit v5 on v4

--- a/solution.py
+++ b/solution.py
@@ -30,7 +30,7 @@
 
 
 SHARES = (12, 12, 12)
-HALO = (8, 16, 8)
+HALO = (8, 14, 8)
 
 
 def chunks_of(per, slots):

time: 40.5 us -> 40 us (0.988)
  Pallas kernels: 39.4 us -> 38.9 us
    pallas_call x1, Pallas kernels: 39.4 us -> 38.9 us  [body(): pl.pallas_call(functools.partial(kernel, (dirs, nears, per, slots, chunks...]
where the time goes in v5:
time: 40 us; the launch traced here: 39.9 us
  Pallas kernels  38.9 us (97%)
  local copies, waits for them, and re-layouts  0.97 us (2%)
    pallas_call x1, Pallas kernels, body(): pl.pallas_call(functools.partial(kernel, (dirs, nears, per, slots, chunks...  38.9 us
    unnamed x1, local copies, waits for them, and re-layouts  0.97 us

profile of v5, /device:TPU:0, one launch (start us, length us, event | category | flops | bytes accessed | tf_op | source)
XLA Modules:
  0.0 39.9 jit_solution(13248049289064745348)
XLA Ops:
  0.0 38.9 %shard_map.73 = bf16[32,128,128]{2,1,0:T(8,128)(2,1)S(1)} custom-call(s32[32]{0:T(128)} %refs_0_.1, s32[6,32]{1,0:T(8,128)} %bitcast.1, bf16[32,128,128]{2,1,0:T(8,128)(2,1)} %refs_2_.1, bf16[32,6,128,256]{3,2,1,0:T(8,128)(2,1)} %refs_3_.1, bf16[8,1152,256]{2,1,0:T(8,128)(2,1)} %refs_4_.1, bf16[8,128,2304]{2,1,0:T(8,128)(2,1)} %refs_5_.1, ...), custom_call_target="tpu_custom_call" | custom-call | tf_op jit(solution)/shard_map/pallas_call | solution.py:540
  38.9 1.0 %copy.9 = bf16[32,128,128]{2,1,0:T(8,128)(2,1)} copy(bf16[32,128,128]{2,1,0:T(8,128)(2,1)S(1)} %shard_map.73) | data formatting | bytes 2097152

commit v6 on v5

--- a/solution.py
+++ b/solution.py
@@ -469,7 +469,7 @@
             out[s * CHILDREN + c] = jnp.where(s < own_count, total, 0.0).astype(BF16)
         return carry
 
-    lax.fori_loop(0, CHILDREN, finish, 0)
+    lax.fori_loop(0, CHILDREN, finish, 0, unroll=True)
 
     to_mate.wait_send()
     for p in range(pieces):

time: 40 us -> 40 us (level)
  no operation moved by 1% of the time
where the time goes in v6:
time: 40 us; the launch traced here: 39.9 us
  Pallas kernels  38.9 us (97%)
  local copies, waits for them, and re-layouts  0.97 us (2%)
    pallas_call x1, Pallas kernels, body(): pl.pallas_call(functools.partial(kernel, (dirs, nears, per, slots, chunks...  38.9 us
    unnamed x1, local copies, waits for them, and re-layouts  0.97 us

profile of v6, /device:TPU:0, one launch (start us, length us, event | category | flops | bytes accessed | tf_op | source)
XLA Modules:
  0.0 39.9 jit_solution(7803853387021335270)
XLA Ops:
  0.0 38.9 %shard_map.73 = bf16[32,128,128]{2,1,0:T(8,128)(2,1)S(1)} custom-call(s32[32]{0:T(128)} %refs_0_.1, s32[6,32]{1,0:T(8,128)} %bitcast.1, bf16[32,128,128]{2,1,0:T(8,128)(2,1)} %refs_2_.1, bf16[32,6,128,256]{3,2,1,0:T(8,128)(2,1)} %refs_3_.1, bf16[8,1152,256]{2,1,0:T(8,128)(2,1)} %refs_4_.1, bf16[8,128,2304]{2,1,0:T(8,128)(2,1)} %refs_5_.1, ...), custom_call_target="tpu_custom_call" | custom-call | tf_op jit(solution)/shard_map/pallas_call | solution.py:540
  38.9 1.0 %copy.9 = bf16[32,128,128]{2,1,0:T(8,128)(2,1)} copy(bf16[32,128,128]{2,1,0:T(8,128)(2,1)S(1)} %shard_map.73) | data formatting | bytes 2097152
